TPU v7x, 512 devices: a whole 4x8x8 slice. The times are simulated.
512 devices in a mesh: node: 64 (over y_lo, z, core), win: 8 (over y_hi, x).
Axes of the slice: x: 4, y: 8 (y_hi: 2, y_lo: 4; y = y_hi * 4 + y_lo), z: 8, core: 2. Of those that a mesh axis runs over, the one named last changes fastest.
Arguments:
- features: bfloat16 [32768, 8, 2, 128], P('node', 'win'), may hold values from -6 to 6
- node_vectors: float32 [32768, 128], P('node'), may hold values from -0.3 to 0.3
- projections: float32 [2, 64, 64], replicated, may hold values from -0.75 to 0.75
- mix_weight: bfloat16 [3, 128, 128], replicated, may hold values from -0.3125 to 0.3125
- region_sizes: int32 [128], replicated, may hold values from 1 to 4, 256 in all
- cotangent: bfloat16 [32768, 8, 2, 128], P('node', 'win'), may hold values from -6 to 6
Outputs:
- layer_output: bfloat16 [32768, 8, 2, 128], P('node', 'win')
- vector_grad: float32 [32768, 128], P('node')
- weight_grad: float32 [3, 128, 128], replicated
Inputs may be any that keep to these rules, and one draw needn't show every extreme that they name: `region_sizes`: each entry is a region size in units of 128 nodes; the entries sum to 256, and the largest region has 512 nodes.
All inputs are finite; a program needn't handle non-finite values.
Results may differ from a plain program's by a relative error of at most 0.015.
Values may be sent and summed in bfloat16 or wider, within the bound.
No kernel may reach another device: no remote copies, remote signals or barrier semaphores. Data moves between devices by JAX's collectives and lax.ppermute only.
A program may use at most 64 MiB of HBM per device.

v0:
```python
from functools import partial
import math
import jax
import jax.numpy as jnp
from jax import lax
from jax.sharding import PartitionSpec as P

BLOCK = 128
KEEP_INPUT = 0.05
ROWS_DIMS = (((1,), (1,)), ((), ()))
COLS_DIMS = (((0,), (0,)), ((), ()))


def padded(cells, sides, width):
    for axis, dim in sides:
        count = lax.axis_size(axis)
        ends = count - 1
        head = lax.slice_in_dim(cells, 0, width, axis=dim)
        tail = lax.slice_in_dim(cells, cells.shape[dim] - width, cells.shape[dim], axis=dim)
        cells = jnp.concatenate(
            [
                lax.ppermute(tail, axis, [(i, (i + 1) % count) for i in range(ends)]),
                cells,
                lax.ppermute(head, axis, [((i + 1) % count, i) for i in range(ends)]),
            ],
            axis=dim,
        )
    return cells


def shifted(block, axis, distance):
    devices = range(lax.axis_size(axis))
    route = [(i - distance, i) for i in devices if i - distance in devices]
    return lax.ppermute(block, axis, route)


def swapped(vectors):
    emb_half = vectors.shape[1] // 2
    return jnp.concatenate([vectors[:, emb_half:], -vectors[:, :emb_half]], axis=1)


def node_regions(region_sizes, node_index, node_total):
    region_ends = jnp.cumsum(region_sizes) * BLOCK
    region_index = jnp.sum((region_ends[None, :] <= node_index[:, None]).astype(jnp.int32), axis=1)
    in_range = (node_index >= 0) & (node_index < node_total)
    return jnp.where(in_range, region_index, -1)


def node_rim(values):
    return padded(values, (("node", 0),), values.shape[0])


def node_pass(values, offset_by):
    return shifted(values.astype(jnp.bfloat16), "node", offset_by).astype(values.dtype)


def spread_back(parts, node_count):
    lower = parts[:node_count]
    middle = parts[node_count : 2 * node_count]
    upper = parts[2 * node_count :]
    return middle + node_pass(lower, -1) + node_pass(upper, 1)


def dense_product(adj_rounded, wide_rows):
    return jnp.dot(adj_rounded, wide_rows, preferred_element_type=jnp.float32)


def body(features, node_vectors, projections, mix_weight, region_sizes, cotangent):
    node_count = features.shape[0]
    windows_dev = features.shape[1]
    steps_dev = features.shape[2]
    channels = features.shape[3]
    row_width = windows_dev * steps_dev * channels
    emb_half = node_vectors.shape[1] // 2
    node_total = node_count * lax.axis_size("node")
    first_node = lax.axis_index("node") * node_count
    own_index = first_node + jnp.arange(node_count, dtype=jnp.int32)
    wide_index = first_node - node_count + jnp.arange(3 * node_count, dtype=jnp.int32)
    own_region = node_regions(region_sizes, own_index, node_total)
    wide_region = node_regions(region_sizes, wide_index, node_total)
    highest = lax.Precision.HIGHEST
    source_m = jnp.tanh(
        3.0
        * jnp.dot(
            node_vectors[:, :emb_half],
            projections[0],
            precision=highest,
            preferred_element_type=jnp.float32,
        )
    )
    target_m = jnp.tanh(
        3.0
        * jnp.dot(
            node_vectors[:, emb_half:],
            projections[1],
            precision=highest,
            preferred_element_type=jnp.float32,
        )
    )
    learned = jnp.concatenate([source_m, target_m], axis=1).astype(jnp.bfloat16)
    inputs = features.reshape(node_count, row_width)
    rim_block = node_rim(jnp.concatenate([inputs, learned], axis=1))
    wide_inputs = rim_block[:, :row_width]
    wide_learned = rim_block[:, row_width:]
    scores = lax.dot_general(
        learned, swapped(wide_learned), ROWS_DIMS, preferred_element_type=jnp.float32
    )
    same_region = (own_region[:, None] == wide_region[None, :]) & (wide_region[None, :] >= 0)
    squashed = jnp.tanh(3.0 * scores)
    positive = jnp.maximum(squashed, 0.0)
    adjacency = jnp.where(same_region, positive * positive, 0.0)
    degree = 1.0 + jnp.sum(adjacency, axis=1)
    identity = (own_index[:, None] == wide_index[None, :]).astype(jnp.float32)
    adj_rounded = (adjacency + identity).astype(jnp.bfloat16)
    propagate = partial(dense_product, adj_rounded)
    inputs_f = inputs.astype(jnp.float32)
    prop_one = propagate(wide_inputs) / degree[:, None]
    hop_one = (KEEP_INPUT * inputs_f + (1.0 - KEEP_INPUT) * prop_one).astype(jnp.bfloat16)
    wide_one = node_rim(hop_one)
    prop_two = propagate(wide_one) / degree[:, None]
    hop_two = (KEEP_INPUT * inputs_f + (1.0 - KEEP_INPUT) * prop_two).astype(jnp.bfloat16)
    row_count = node_count * windows_dev * steps_dev
    hop_list = (inputs, hop_one, hop_two)
    mixed = jnp.zeros((row_count, channels), jnp.float32)
    for hop_order in range(3):
        mixed = mixed + jnp.dot(
            hop_list[hop_order].reshape(row_count, channels),
            mix_weight[hop_order],
            preferred_element_type=jnp.float32,
        )
    layer_output = mixed.astype(jnp.bfloat16).reshape(features.shape)
    upstream = cotangent.reshape(row_count, channels)
    norm_scale = 1.0 / math.sqrt(row_count * lax.axis_size("node") * lax.axis_size("win"))
    partial_mix = (
        jnp.stack(
            [
                lax.dot_general(
                    layer_rows.reshape(row_count, channels),
                    upstream,
                    COLS_DIMS,
                    preferred_element_type=jnp.float32,
                )
                for layer_rows in hop_list
            ]
        )
        * norm_scale
    )
    weight_grad = lax.psum(partial_mix, ("node", "win"))
    back_two = lax.dot_general(
        upstream, mix_weight[2], ROWS_DIMS, preferred_element_type=jnp.float32
    ).reshape(node_count, row_width)
    grad_two = ((1.0 - KEEP_INPUT) * back_two / degree[:, None]).astype(jnp.bfloat16)
    partials = lax.dot_general(adj_rounded, grad_two, COLS_DIMS, preferred_element_type=jnp.float32)
    carried = spread_back(partials, node_count)
    back_one = (
        lax.dot_general(
            upstream, mix_weight[1], ROWS_DIMS, preferred_element_type=jnp.float32
        ).reshape(node_count, row_width)
        + carried
    )
    grad_one = ((1.0 - KEEP_INPUT) * back_one / degree[:, None]).astype(jnp.bfloat16)
    pair_inner = lax.dot_general(
        jnp.concatenate([grad_one, grad_two], axis=1),
        jnp.concatenate([wide_inputs, wide_one], axis=1),
        ROWS_DIMS,
        preferred_element_type=jnp.float32,
    )
    offset = jnp.sum(grad_one.astype(jnp.float32) * prop_one, axis=1) + jnp.sum(
        grad_two.astype(jnp.float32) * prop_two, axis=1
    )
    score_grad = jnp.where(
        same_region,
        6.0 * (pair_inner - offset[:, None]) * positive * (1.0 - squashed * squashed),
        0.0,
    ).astype(jnp.bfloat16)
    row_part = jnp.dot(score_grad, swapped(wide_learned), preferred_element_type=jnp.float32)
    column_part = -lax.dot_general(
        score_grad, swapped(learned), COLS_DIMS, preferred_element_type=jnp.float32
    )
    grad_m = row_part + spread_back(column_part, node_count)
    source_grad = jnp.dot(
        3.0 * (1.0 - source_m * source_m) * grad_m[:, :emb_half],
        projections[0].T,
        precision=highest,
        preferred_element_type=jnp.float32,
    )
    target_grad = jnp.dot(
        3.0 * (1.0 - target_m * target_m) * grad_m[:, emb_half:],
        projections[1].T,
        precision=highest,
        preferred_element_type=jnp.float32,
    )
    vector_grad = lax.psum(
        jnp.concatenate([source_grad, target_grad], axis=1).astype(jnp.bfloat16), "win"
    ).astype(jnp.float32)
    return (layer_output, vector_grad, weight_grad)


def solution(mesh):
    placed = (
        P("node", "win", None, None),
        P("node", None),
        P(),
        P(),
        P(),
        P("node", "win", None, None),
    )
    return jax.shard_map(
        body,
        mesh=mesh,
        in_specs=placed,
        out_specs=(P("node", "win", None, None), P("node", None), P()),
        check_vma=False,
    )
```

profile of v0, /device:TPU:1, one launch (start us, length us, event | category | flops | bytes accessed | tf_op | source)
XLA Modules:
  0.0 480.1 jit_solution(4617464330748801811)
XLA Ops:
  7.2 0.0 copy-start
  7.2 0.0 all-reduce.3.cloned.1.call-start
  7.2 2.1 fusion.88
  9.4 2.1 fusion.83
  11.4 0.1 copy.31
  11.6 1.0 copy.51
  12.6 0.1 copy.30
  12.7 0.1 pad_maximum_fusion.1
  12.8 8.8 %collective-permute-start.1 = (bf16[512,384]{1,0:T(8,128)(2,1)S(1)}, bf16[512,384]{1,0:T(8,128)(2,1)S(1)}, u32[]{:S(2)}, u32[]{:S(2)}) collective-permute-start(bf16[512,384]{1,0:T(8,128)(2,1)S(1)} %pad_maximum_fusion.1), channel_id=1, source_target_pairs={{8,0},{16,8},{24,16},{32,24},{40,32},{48,40},{56,48},{64,56},{72,6... | collective-permute-start | bytes 1179656 | tf_op jit(solution)/shard_map/ppermute | solution.py:24
  21.6 1.9 collective-permute-start
  23.5 0.1 copy.29
  23.7 0.2 reduce-window.8
  23.8 0.1 multiply_reduce_fusion.2
  23.9 0.2 convert_reduce_fusion.1
  24.2 0.5 convert_reduce_fusion
  24.7 1.0 convolution_multiply_fusion.1
  25.7 2.5 collective-permute-done
  28.2 0.2 pad_maximum_fusion
  28.4 0.2 fusion.85
  28.6 0.0 copy-start.8
  28.6 3.3 fusion.6
  32.0 0.0 copy-start.14
  32.0 1.5 add_convert_fusion.2
  33.5 1.9 collective-permute-start.3
  35.4 4.4 collective-permute-start.2
  39.8 0.2 fusion.55
  40.1 0.1 mul.107
  40.2 1.0 fusion.62
  41.2 1.0 collective-permute-done.3
  42.3 1.2 collective-permute-done.2
  43.4 3.5 multiply_reduce_fusion
  46.9 0.6 fusion.89
  47.5 0.8 fusion.86
  48.4 1.9 collective-permute-start.4
  50.3 4.4 collective-permute-start.5
  54.7 0.9 convolution_bitcast_fusion.2
  55.6 0.9 reshape.110
  56.6 1.1 reshape.106
  57.7 2.2 convolution_add_fusion.1
  59.9 1.6 multiply_reduce_fusion.1
  61.6 2.9 fusion.5
  64.5 0.0 copy-start.18
  64.6 1.3 fusion.90
  65.8 0.7 fusion.87
  66.6 2.0 collective-permute-start.6
  68.6 3.6 collective-permute-start.7
  72.3 0.9 convolution_bitcast_fusion.1
  73.1 0.1 reshape.107
  73.3 1.2 collective-permute-done.7
  74.5 0.7 copy-done.21
  75.2 2.0 fusion.31
  77.2 1.1 convolution_convert_fusion
  78.2 1.0 convolution_convert_fusion.1
  79.3 0.7 pad_maximum_fusion.3
  80.0 0.0 all-reduce.3.cloned.1.call-update
  80.0 0.0 all-reduce.5.cloned.1.call-start
  80.0 0.3 convolution_bitcast_fusion
  80.3 0.7 maximum_multiply_fusion
  81.0 0.0 all-reduce.5.cloned.1.call-update
  81.1 1.7 fusion.14
  82.7 113.3 %all-reduce.3.cloned.1.call-done = bf16[512,128]{0,1:T(8,128)(2,1)} async-done(((bf16[512,128]{0,1:T(8,128)(2,1)}), bf16[512,128]{0,1:T(8,128)(2,1)}) %all-reduce.3.cloned.1.call-update) | async-done | bytes 131088 | tf_op jit(solution)/shard_map/psum | solution.py:193
  196.0 1.7 copy.38
  197.8 273.9 %all-reduce.5.cloned.1.call-done = f32[3,128,128]{2,1,0:T(8,128)} async-done(((f32[3,128,128]{2,1,0:T(8,128)}), f32[3,128,128]{2,1,0:T(8,128)}) %all-reduce.5.cloned.1.call-update) | async-done | bytes 196624 | tf_op jit(solution)/shard_map/psum | solution.py:148
  471.7 1.6 copy.54
  (63 shorter events, 0.2 us)
Async XLA Ops:
  7.2 17.5 %copy-start = (bf16[512,1,2,128]{3,2,1,0:T(2,128)(2,1)S(1)}, bf16[512,1,2,128]{3,2,1,0:T(2,128)(2,1)}, u32[]{:S(2)}) copy-start(bf16[512,1,2,128]{3,2,1,0:T(2,128)(2,1)} %param.11) | copy-start | bytes 786436
  7.2 16.4 %copy-start.26 = (s32[128]{0:T(128)S(1)}, s32[128]{0:T(128)}, u32[]{:S(2)}) copy-start(s32[128]{0:T(128)} %param.10) | copy-start | bytes 1540
  7.2 188.9 %all-reduce.3.cloned.1.call-start = ((), (), s32[]{:S(2)}) async-start(), calls=%async_computation | async-start | bytes 262144 | tf_op jit(solution)/shard_map/psum | solution.py:193
  9.4 19.2 %copy-start.10 = (bf16[512,64]{0,1:T(8,128)(2,1)}, bf16[512,64]{0,1:T(8,128)(2,1)S(1)}, u32[]{:S(2)}) copy-start(bf16[512,64]{0,1:T(8,128)(2,1)S(1)} %get-tuple-element.29) | copy-start | bytes 196612
  12.8 12.9 %collective-permute-start.1 = (bf16[512,384]{1,0:T(8,128)(2,1)S(1)}, bf16[512,384]{1,0:T(8,128)(2,1)S(1)}, u32[]{:S(2)}, u32[]{:S(2)}) collective-permute-start(bf16[512,384]{1,0:T(8,128)(2,1)S(1)} %pad_maximum_fusion.1), channel_id=1, source_target_pairs={{8,0},{16,8},{24,16},{32,24},{40,32},{48,40},{56,48},{64,56},{72,6... | collective-permute-start | bytes 1179656 | tf_op jit(solution)/shard_map/ppermute | solution.py:24
  21.6 6.6 %collective-permute-start = (bf16[512,384]{1,0:T(8,128)(2,1)S(1)}, bf16[512,384]{1,0:T(8,128)(2,1)S(1)}, u32[]{:S(2)}, u32[]{:S(2)}) collective-permute-start(bf16[512,384]{1,0:T(8,128)(2,1)S(1)} %pad_maximum_fusion.1), channel_id=1, source_target_pairs={{0,8},{8,16},{16,24},{24,32},{32,40},{40,48},{48,56},{56,64},{64,7... | collective-permute-start | bytes 1179656 | tf_op jit(solution)/shard_map/ppermute | solution.py:22
  24.7 3.9 copy-start.24
  28.4 28.2 %copy-start.1 = (bf16[1536,384]{1,0:T(8,128)(2,1)}, bf16[1536,384]{1,0:T(8,128)(2,1)S(1)}, u32[]{:S(2)}) copy-start(bf16[1536,384]{1,0:T(8,128)(2,1)S(1)} %pad_maximum_fusion) | copy-start | bytes 3538948
  28.6 3.4 copy-start.3
  28.6 3.4 copy-start.5
  28.6 3.4 copy-start.8
  32.0 1.5 copy-start.6
  32.0 7.8 %copy-start.14 = (bf16[3,128,128]{2,1,0:T(8,128)(2,1)S(1)}, bf16[3,128,128]{2,1,0:T(8,128)(2,1)}, u32[]{:S(2)}) copy-start(bf16[3,128,128]{2,1,0:T(8,128)(2,1)} %param.9) | copy-start | bytes 294916
  33.5 8.7 %collective-permute-start.3 = (bf16[512,256]{1,0:T(8,128)(2,1)}, bf16[512,256]{1,0:T(8,128)(2,1)}, u32[]{:S(2)}, u32[]{:S(2)}) collective-permute-start(bf16[512,256]{1,0:T(8,128)(2,1)} %get-tuple-element.33), channel_id=1, source_target_pairs={{8,0},{16,8},{24,16},{32,24},{40,32},{48,40},{56,48},{64,56},{72,6... | collective-permute-start | bytes 786440 | tf_op jit(solution)/shard_map/ppermute | solution.py:24
  35.4 8.0 %collective-permute-start.2 = (bf16[512,256]{1,0:T(8,128)(2,1)}, bf16[512,256]{1,0:T(8,128)(2,1)}, u32[]{:S(2)}, u32[]{:S(2)}) collective-permute-start(bf16[512,256]{1,0:T(8,128)(2,1)} %get-tuple-element.33), channel_id=1, source_target_pairs={{0,8},{8,16},{16,24},{24,32},{32,40},{40,48},{48,56},{56,64},{64,7... | collective-permute-start | bytes 786440 | tf_op jit(solution)/shard_map/ppermute | solution.py:22
  41.2 5.7 %copy-start.7 = (bf16[512,1536]{1,0:T(8,128)(2,1)S(1)}, bf16[512,1536]{1,0:T(8,128)(2,1)}, u32[]{:S(2)}) copy-start(bf16[512,1536]{1,0:T(8,128)(2,1)} %copy-done.6) | copy-start | bytes 4718596
  46.9 1.5 copy-start.15
  46.9 7.8 %copy-start.9 = (bf16[512,1,2,128]{3,2,1,0:T(2,128)(2,1)S(1)}, bf16[512,1,2,128]{3,2,1,0:T(2,128)(2,1)}, u32[]{:S(2)}) copy-start(bf16[512,1,2,128]{3,2,1,0:T(2,128)(2,1)} %param.6) | copy-start | bytes 786436
  48.4 11.6 %collective-permute-start.4 = (bf16[512,256]{1,0:T(8,128)(2,1)}, bf16[512,256]{1,0:T(8,128)(2,1)}, u32[]{:S(2)}, u32[]{:S(2)}) collective-permute-start(bf16[512,256]{1,0:T(8,128)(2,1)} %get-tuple-element.24), channel_id=1, source_target_pairs={{8,0},{16,8},{24,16},{32,24},{40,32},{48,40},{56,48},{64,56},{72,6... | collective-permute-start | bytes 786440 | tf_op jit(solution)/shard_map/ppermute | solution.py:34
  50.3 9.6 %collective-permute-start.5 = (bf16[512,256]{1,0:T(8,128)(2,1)}, bf16[512,256]{1,0:T(8,128)(2,1)}, u32[]{:S(2)}, u32[]{:S(2)}) collective-permute-start(bf16[512,256]{1,0:T(8,128)(2,1)} %get-tuple-element.25), channel_id=1, source_target_pairs={{0,8},{8,16},{16,24},{24,32},{32,40},{40,48},{48,56},{56,64},{64,7... | collective-permute-start | bytes 786440 | tf_op jit(solution)/shard_map/ppermute | solution.py:34
  56.5 5.0 %copy-start.23 = (f32[512]{0:T(512)S(1)}, f32[512]{0:T(512)}, u32[]{:S(2)}) copy-start(f32[512]{0:T(512)} %get-tuple-element.14) | copy-start | bytes 6148
  56.5 5.0 %slice-start = ((bf16[1536,384]{1,0:T(8,128)(2,1)}), bf16[1536,256]{1,0:T(8,128)(2,1)S(1)}, s32[]{:S(2)}) async-start(bf16[1536,384]{1,0:T(8,128)(2,1)} %copy-done.1), calls=%async_computation.2 | async-start | bytes 1572864 | tf_op jit(solution)/shard_map/slice | solution.py:103
  56.5 5.0 %copy-start.16 = (bf16[512,256]{1,0:T(8,128)(2,1)S(1)}, bf16[512,256]{1,0:T(8,128)(2,1)}, u32[]{:S(2)}) copy-start(bf16[512,256]{1,0:T(8,128)(2,1)} %copy-done.15) | copy-start | bytes 786436
  57.7 3.9 copy-start.25
  57.7 3.9 copy-start.27
  61.6 2.9 copy-start.11
  61.6 2.9 copy-start.17
  64.5 8.6 %copy-start.18 = (bf16[512,256]{1,0:T(8,128)(2,1)S(1)}, bf16[512,256]{1,0:T(8,128)(2,1)}, u32[]{:S(2)}) copy-start(bf16[512,256]{1,0:T(8,128)(2,1)} %get-tuple-element.26) | copy-start | bytes 786436
  64.5 10.6 %copy-start.4 = (bf16[1536,64]{1,0:T(8,128)(2,1)S(1)}, bf16[1536,64]{1,0:T(8,128)(2,1)}, u32[]{:S(2)}) copy-start(bf16[1536,64]{1,0:T(8,128)(2,1)} %copy-done.3) | copy-start | bytes 589828
  65.8 11.3 %copy-start.13 = (f32[512,64]{0,1:T(8,128)S(1)}, f32[512,64]{0,1:T(8,128)}, u32[]{:S(2)}) copy-start(f32[512,64]{0,1:T(8,128)} %get-tuple-element.30) | copy-start | bytes 393220
  66.6 11.7 %copy-start.12 = (f32[512,64]{0,1:T(8,128)S(1)}, f32[512,64]{0,1:T(8,128)}, u32[]{:S(2)}) copy-start(f32[512,64]{0,1:T(8,128)} %get-tuple-element.31) | copy-start | bytes 393220
  66.6 6.7 %collective-permute-start.6 = (bf16[512,128]{0,1:T(8,128)(2,1)}, bf16[512,128]{0,1:T(8,128)(2,1)S(1)}, u32[]{:S(2)}, u32[]{:S(2)}) collective-permute-start(bf16[512,128]{0,1:T(8,128)(2,1)} %get-tuple-element.27), channel_id=1, source_target_pairs={{8,0},{16,8},{24,16},{32,24},{40,32},{48,40},{56,48},{64,56},{72,6... | collective-permute-start | bytes 393224 | tf_op jit(solution)/shard_map/ppermute | solution.py:34
  68.6 5.9 %collective-permute-start.7 = (bf16[512,128]{0,1:T(8,128)(2,1)}, bf16[512,128]{0,1:T(8,128)(2,1)S(1)}, u32[]{:S(2)}, u32[]{:S(2)}) collective-permute-start(bf16[512,128]{0,1:T(8,128)(2,1)} %get-tuple-element.28), channel_id=1, source_target_pairs={{0,8},{8,16},{16,24},{24,32},{32,40},{40,48},{48,56},{56,64},{64,7... | collective-permute-start | bytes 393224 | tf_op jit(solution)/shard_map/ppermute | solution.py:34
  73.2 1.2 copy-start.20
  74.5 0.7 copy-start.21
  75.2 5.1 %copy-start.19 = (f32[1,128,128]{2,1,0:T(8,128)S(1)}, f32[1,128,128]{2,1,0:T(8,128)}, u32[]{:S(2)}) copy-start(f32[1,128,128]{2,1,0:T(8,128)} %convolution_bitcast_fusion.1) | copy-start | bytes 196612
  75.2 5.2 %copy-start.22 = (f32[1,128,128]{2,1,0:T(8,128)S(1)}, f32[1,128,128]{2,1,0:T(8,128)}, u32[]{:S(2)}) copy-start(f32[1,128,128]{2,1,0:T(8,128)} %convolution_bitcast_fusion.2) | copy-start | bytes 196612
  75.2 5.9 %copy-start.2 = (f32[1024,128]{1,0:T(8,128)S(1)}, f32[1024,128]{1,0:T(8,128)}, u32[]{:S(2)}) copy-start(f32[1024,128]{1,0:T(8,128)} %convolution_add_fusion.1) | copy-start | bytes 1572868
  80.0 391.7 %all-reduce.5.cloned.1.call-start = ((), (), s32[]{:S(2)}) async-start(), calls=%async_computation.1 | async-start | bytes 393216 | tf_op jit(solution)/shard_map/psum | solution.py:148
Sparse Core Ops, SparseCore 0:
  80.1 115.9 all-reduce.2
  201.6 270.0 all-reduce.4
where the time goes:
time: 481 us; the launch traced here: 480 us
  waiting for transfers between devices  393 us (82%)
  matrix products  29.5 us (6%)
  starting transfers between devices  29 us (6%)
  between operations  14.6 us (3%)
  local copies, waits for them, and re-layouts  9.33 us (2%)
    psum x1, waiting for transfers between devices, body(): weight_grad = lax.psum(partial_mix, ('node', 'win'))  274 us
    psum x1, waiting for transfers between devices, body(): lax.psum(jnp.concatenate([source_grad, target_grad], axis=1).astype(jnp.b...  113 us
    ppermute x4, starting transfers between devices, shifted(): return lax.ppermute(block, axis, route)  12 us
    ppermute x2, starting transfers between devices, padded(): lax.ppermute(head, axis, [((i + 1) % count, i) for i in range(ends)])  10.7 us
  transfers between devices with their start and end apart: 10, of which 6 were waited for; matrix products, arithmetic and copies ran while one was open for 3% of the time, Pallas kernels for 0%

commit v1 on v0

--- a/solution.py
+++ b/solution.py
@@ -145,7 +145,9 @@
         )
         * norm_scale
     )
-    weight_grad = lax.psum(partial_mix, ("node", "win"))
+    weight_grad = partial_mix
+    for name in ("node", "win"):
+        weight_grad = lax.psum(weight_grad, name)
     back_two = lax.dot_general(
         upstream, mix_weight[2], ROWS_DIMS, preferred_element_type=jnp.float32
     ).reshape(node_count, row_width)

time: 481 us -> 800 us (1.66)
  waiting for transfers between devices: 393 us -> 708 us
    psum x1 -> x2, waiting for transfers between devices: 274 us -> 597 us  [body(): weight_grad = lax.psum(weight_grad, name)]
  transfers between devices with their start and end apart: 10 -> 11, of which waited for: 6 -> 6; matrix products, arithmetic and copies ran while one was open for 3% -> 2% of each run, Pallas kernels for 0% -> 0%
where the time goes in v1:
time: 800 us; the launch traced here: 795 us
  waiting for transfers between devices  708 us (88%)
  starting transfers between devices  29.3 us (4%)
  matrix products  29 us (4%)
  between operations  14.2 us (2%)
  local copies, waits for them, and re-layouts  10.3 us (1%)
    psum x2, waiting for transfers between devices, body(): weight_grad = lax.psum(weight_grad, name)  597 us
    psum x1, waiting for transfers between devices, body(): lax.psum(jnp.concatenate([source_grad, target_grad], axis=1).astype(jnp.b...  106 us
  transfers between devices with their start and end apart: 11, of which 6 were waited for; matrix products, arithmetic and copies ran while one was open for 2% of the time, Pallas kernels for 0%

profile of v1, /device:TPU:1, one launch (start us, length us, event | category | flops | bytes accessed | tf_op | source)
XLA Modules:
  0.0 795.0 jit_solution(5362295032494315795)
XLA Ops:
  7.2 0.0 copy-start
  7.2 0.0 all-reduce.6.cloned.1.call-start
  7.2 2.2 fusion.88
  9.4 2.1 fusion.83
  11.5 0.1 copy.31
  11.6 1.0 copy.51
  12.6 0.1 copy.30
  12.7 0.1 pad_maximum_fusion.1
  12.9 8.7 %collective-permute-start.1 = (bf16[512,384]{1,0:T(8,128)(2,1)S(1)}, bf16[512,384]{1,0:T(8,128)(2,1)S(1)}, u32[]{:S(2)}, u32[]{:S(2)}) collective-permute-start(bf16[512,384]{1,0:T(8,128)(2,1)S(1)} %pad_maximum_fusion.1), channel_id=1, source_target_pairs={{8,0},{16,8},{24,16},{32,24},{40,32},{48,40},{56,48},{64,56},{72,6... | collective-permute-start | bytes 1179656 | tf_op jit(solution)/shard_map/ppermute | solution.py:24
  21.6 1.9 collective-permute-start
  23.6 0.1 copy.29
  23.7 0.2 reduce-window.8
  23.9 0.1 multiply_reduce_fusion.2
  24.0 0.2 convert_reduce_fusion.1
  24.2 0.5 convert_reduce_fusion
  24.8 0.2 convolution_multiply_fusion.1
  25.0 3.2 collective-permute-done
  28.2 0.2 pad_maximum_fusion
  28.4 0.2 fusion.85
  28.7 0.0 copy-start.8
  28.7 3.3 fusion.6
  32.0 1.4 add_convert_fusion.2
  33.5 1.9 collective-permute-start.3
  35.4 4.4 collective-permute-start.2
  39.8 0.2 fusion.55
  40.0 1.0 mul.107
  41.0 0.9 reshape.110
  41.9 1.0 fusion.62
  42.9 0.1 collective-permute-done.2
  43.1 3.6 multiply_reduce_fusion
  46.7 0.6 fusion.89
  47.3 0.8 fusion.86
  48.2 1.9 collective-permute-start.4
  50.1 4.3 collective-permute-start.5
  54.4 0.9 convolution_bitcast_fusion.2
  55.3 1.1 reshape.106
  56.4 0.9 convolution_bitcast_fusion.1
  57.3 1.0 reshape.107
  58.4 1.6 multiply_reduce_fusion.1
  60.0 0.0 copy-start.13
  60.0 4.0 fusion.5
  64.1 1.3 fusion.90
  65.3 0.7 fusion.87
  66.0 1.9 collective-permute-start.6
  68.0 4.0 collective-permute-start.7
  72.0 0.3 convolution_bitcast_fusion
  72.3 0.7 maximum_multiply_fusion
  73.0 0.0 all-reduce.6.cloned.1.call-update
  73.0 0.0 all-reduce.4.cloned.1.call-start
  73.1 1.1 collective-permute-done.7
  74.3 1.9 fusion.31
  76.2 1.2 convolution_convert_fusion
  77.4 1.2 convolution_convert_fusion.1
  78.6 0.7 pad_maximum_fusion.3
  79.3 0.0 all-reduce.4.cloned.1.call-update
  79.3 0.0 all-reduce.8.cloned.1.call-start
  79.3 1.0 convolution_add_fusion.1
  80.3 487.6 %all-reduce.6.cloned.1.call-done = f32[3,128,128]{2,1,0:T(8,128)} async-done(((f32[3,128,128]{2,1,0:T(8,128)}), f32[3,128,128]{2,1,0:T(8,128)}) %all-reduce.6.cloned.1.call-update) | async-done | bytes 196624 | tf_op jit(solution)/shard_map/psum | solution.py:150
  568.0 0.0 all-reduce.8.cloned.1.call-update
  568.0 1.7 fusion.14
  569.7 106.3 %all-reduce.4.cloned.1.call-done = bf16[512,128]{0,1:T(8,128)(2,1)} async-done(((bf16[512,128]{0,1:T(8,128)(2,1)}), bf16[512,128]{0,1:T(8,128)(2,1)}) %all-reduce.4.cloned.1.call-update) | async-done | bytes 131088 | tf_op jit(solution)/shard_map/psum | solution.py:195
  676.0 1.7 copy.38
  677.7 109.2 %all-reduce.8.cloned.1.call-done = f32[3,128,128]{2,1,0:T(8,128)} async-done(((f32[3,128,128]{2,1,0:T(8,128)}), f32[3,128,128]{2,1,0:T(8,128)}) %all-reduce.8.cloned.1.call-update) | async-done | bytes 196624 | tf_op jit(solution)/shard_map/psum | solution.py:150
  786.9 1.6 copy.55
  (54 shorter events, 0.1 us)
Async XLA Ops:
  7.2 17.6 %copy-start = (bf16[512,1,2,128]{3,2,1,0:T(2,128)(2,1)S(1)}, bf16[512,1,2,128]{3,2,1,0:T(2,128)(2,1)}, u32[]{:S(2)}) copy-start(bf16[512,1,2,128]{3,2,1,0:T(2,128)(2,1)} %param.11) | copy-start | bytes 786436
  7.2 16.4 %copy-start.20 = (s32[128]{0:T(128)S(1)}, s32[128]{0:T(128)}, u32[]{:S(2)}) copy-start(s32[128]{0:T(128)} %param.10) | copy-start | bytes 1540
  7.2 17.6 %copy-start.11 = (bf16[3,128,128]{2,1,0:T(8,128)(2,1)S(1)}, bf16[3,128,128]{2,1,0:T(8,128)(2,1)}, u32[]{:S(2)}) copy-start(bf16[3,128,128]{2,1,0:T(8,128)(2,1)} %param.9) | copy-start | bytes 294916
  7.2 560.8 %all-reduce.6.cloned.1.call-start = ((), (), s32[]{:S(2)}) async-start(), calls=%async_computation.1 | async-start | bytes 393216 | tf_op jit(solution)/shard_map/psum | solution.py:150
  9.4 19.2 %copy-start.9 = (bf16[512,64]{0,1:T(8,128)(2,1)}, bf16[512,64]{0,1:T(8,128)(2,1)S(1)}, u32[]{:S(2)}) copy-start(bf16[512,64]{0,1:T(8,128)(2,1)S(1)} %get-tuple-element.29) | copy-start | bytes 196612
  12.9 12.2 %collective-permute-start.1 = (bf16[512,384]{1,0:T(8,128)(2,1)S(1)}, bf16[512,384]{1,0:T(8,128)(2,1)S(1)}, u32[]{:S(2)}, u32[]{:S(2)}) collective-permute-start(bf16[512,384]{1,0:T(8,128)(2,1)S(1)} %pad_maximum_fusion.1), channel_id=1, source_target_pairs={{8,0},{16,8},{24,16},{32,24},{40,32},{48,40},{56,48},{64,56},{72,6... | collective-permute-start | bytes 1179656 | tf_op jit(solution)/shard_map/ppermute | solution.py:24
  21.6 6.6 collective-permute-start
  24.8 3.9 copy-start.19
  28.4 26.9 %copy-start.1 = (bf16[1536,384]{1,0:T(8,128)(2,1)}, bf16[1536,384]{1,0:T(8,128)(2,1)S(1)}, u32[]{:S(2)}) copy-start(bf16[1536,384]{1,0:T(8,128)(2,1)S(1)} %pad_maximum_fusion) | copy-start | bytes 3538948
  28.6 3.4 copy-start.3
  28.6 3.4 copy-start.5
  28.7 3.4 copy-start.8
  32.0 1.4 copy-start.6
  33.5 13.3 %copy-start.14 = (bf16[512,256]{1,0:T(8,128)(2,1)}, bf16[512,256]{1,0:T(8,128)(2,1)S(1)}, u32[]{:S(2)}) copy-start(bf16[512,256]{1,0:T(8,128)(2,1)S(1)} %get-tuple-element.33) | copy-start | bytes 786436
  33.5 9.5 %collective-permute-start.3 = (bf16[512,256]{1,0:T(8,128)(2,1)S(1)}, bf16[512,256]{1,0:T(8,128)(2,1)S(1)}, u32[]{:S(2)}, u32[]{:S(2)}) collective-permute-start(bf16[512,256]{1,0:T(8,128)(2,1)S(1)} %get-tuple-element.33), channel_id=1, source_target_pairs={{8,0},{16,8},{24,16},{32,24},{40,32},{48,40},{56,48},{64,56},{72,6... | collective-permute-start | bytes 786440 | tf_op jit(solution)/shard_map/ppermute | solution.py:24
  35.4 7.7 collective-permute-start.2
  42.9 3.8 copy-start.7
  42.9 3.8 copy-start.21
  46.7 1.4 copy-start.12
  48.2 10.2 %collective-permute-start.4 = (bf16[512,256]{1,0:T(8,128)(2,1)}, bf16[512,256]{1,0:T(8,128)(2,1)}, u32[]{:S(2)}, u32[]{:S(2)}) collective-permute-start(bf16[512,256]{1,0:T(8,128)(2,1)} %get-tuple-element.24), channel_id=1, source_target_pairs={{8,0},{16,8},{24,16},{32,24},{40,32},{48,40},{56,48},{64,56},{72,6... | collective-permute-start | bytes 786440 | tf_op jit(solution)/shard_map/ppermute | solution.py:34
  50.1 8.3 %collective-permute-start.5 = (bf16[512,256]{1,0:T(8,128)(2,1)}, bf16[512,256]{1,0:T(8,128)(2,1)}, u32[]{:S(2)}, u32[]{:S(2)}) collective-permute-start(bf16[512,256]{1,0:T(8,128)(2,1)} %get-tuple-element.25), channel_id=1, source_target_pairs={{0,8},{8,16},{16,24},{24,32},{32,40},{40,48},{48,56},{56,64},{64,7... | collective-permute-start | bytes 786440 | tf_op jit(solution)/shard_map/ppermute | solution.py:34
  55.3 4.7 copy-start.18
  55.3 4.7 slice-start
  60.0 4.0 copy-start.10
  60.0 4.0 copy-start.13
  64.0 8.3 %copy-start.15 = (f32[1,128,128]{2,1,0:T(8,128)S(1)}, f32[1,128,128]{2,1,0:T(8,128)}, u32[]{:S(2)}) copy-start(f32[1,128,128]{2,1,0:T(8,128)} %convolution_bitcast_fusion.1) | copy-start | bytes 196612
  64.0 8.3 %copy-start.17 = (f32[1,128,128]{2,1,0:T(8,128)S(1)}, f32[1,128,128]{2,1,0:T(8,128)}, u32[]{:S(2)}) copy-start(f32[1,128,128]{2,1,0:T(8,128)} %convolution_bitcast_fusion.2) | copy-start | bytes 196612
  64.0 10.2 %copy-start.4 = (bf16[1536,64]{1,0:T(8,128)(2,1)S(1)}, bf16[1536,64]{1,0:T(8,128)(2,1)}, u32[]{:S(2)}) copy-start(bf16[1536,64]{1,0:T(8,128)(2,1)} %copy-done.3) | copy-start | bytes 589828
  66.0 7.0 collective-permute-start.6
  68.0 6.3 collective-permute-start.7
  72.3 7.0 copy-start.2
  73.0 602.9 %all-reduce.4.cloned.1.call-start = ((), (), s32[]{:S(2)}) async-start(), calls=%async_computation | async-start | bytes 262144 | tf_op jit(solution)/shard_map/psum | solution.py:195
  73.1 1.2 copy-start.16
  79.3 707.6 %all-reduce.8.cloned.1.call-start = ((), (), s32[]{:S(2)}) async-start(), calls=%async_computation.2 | async-start | bytes 393216 | tf_op jit(solution)/shard_map/psum | solution.py:150
Sparse Core Ops, SparseCore 0:
  73.2 494.7 all-reduce.5
  571.4 104.4 all-reduce.3
  678.9 107.9 all-reduce.7
